TPU v7x, 32 devices: a whole 2x2x4 slice. The times are simulated.
32 devices in a mesh: gx: 8 (over z, y), gy: 4 (over x, core).
Axes of the slice: x: 2, y: 2, z: 4, core: 2. Of those that a mesh axis runs over, the one named last changes fastest.
Arguments:
- state_in: float32 [5, 16, 32, 32, 128], P(None, None, 'gx', 'gy'), may hold values from -6 to 6
- sponge: float32 [32, 32, 128], P('gx', 'gy'), may hold values from 0.05 to 0.5
- mean_velocity: float32 [3], replicated, may hold values from -0.6 to 0.6
- wall_vector: float32 [5], replicated, may hold values from -3 to 3
- mode_shapes: float32 [16, 8192], P(None, ('gx', 'gy')), may hold values from -6 to 6
- wall_nodes: int32 [4, 32, 128], P(None, 'gx'), may hold values from 0 to 8191
- wall_weights: float32 [4, 32, 128], P(None, 'gx'), may hold values from 0.1 to 1
- wall_count: int32 [32], P('gx'), may hold values from 32 to 128
Outputs:
- state_out: float32 [5, 16, 32, 32, 128], P(None, None, 'gx', 'gy')
- r_factor: float32 [32, 32], replicated
All inputs are finite; a program needn't handle non-finite values.
Results may differ from a plain program's by a relative error of at most 0.00013.
Values sent between devices are 32-bit elements; how exact they have to be, the bound alone decides.
No kernel may reach another device: no remote copies, remote signals or barrier semaphores. Data moves between devices by JAX's collectives and lax.ppermute only.
A program may use at most 192 MiB of HBM per device.

v0:
```python
import math
import jax
import jax.numpy as jnp
import numpy as np
from jax import lax
from jax.sharding import PartitionSpec as P

STEPS = 2
C_SOUND = 1.0
NU_DAMP = 0.25
DT_STEP = 0.4
PULSE_MID = 0.8
PULSE_WIDTH = 0.5


def padded_2(x, sides, width):
    for axis, dim in sides:
        size, length = (lax.axis_size(axis), x.shape[dim])
        up = [(i, (i + 1) % size) for i in range(size - 1)]
        down = [(j, i) for i, j in up]
        last = lax.slice_in_dim(x, length - width, length, axis=dim)
        initial = lax.slice_in_dim(x, 0, width, axis=dim)
        before = lax.ppermute(last, axis, up)
        after = lax.ppermute(initial, axis, down)
        x = jnp.concatenate([before, x, after], axis=dim)
    return x


def pulse(time_now):
    return math.exp(-(((time_now - PULSE_MID) / PULSE_WIDTH) ** 2))


def jacobians(velocity):
    identity = jnp.eye(5, dtype=velocity.dtype)
    matrices = []
    for dimension in range(3):
        coupling = np.zeros((5, 5))
        coupling[0, 1 + dimension] = 1.0
        coupling[1 + dimension, 4] = 1.0
        coupling[4, 1 + dimension] = C_SOUND * C_SOUND
        matrices.append(velocity[dimension] * identity + jnp.asarray(coupling, velocity.dtype))
    return jnp.stack(matrices)


def rates(padded, jacobian, sponge_here, wall_rows, wall_line):
    highest = lax.Precision.HIGHEST
    center = padded[:, :, 1:-1, 1:-1, :]
    east_side = padded[:, :, 2:, 1:-1, :]
    west_side = padded[:, :, :-2, 1:-1, :]
    north_side = padded[:, :, 1:-1, 2:, :]
    south_side = padded[:, :, 1:-1, :-2, :]
    zero_plane = jnp.zeros_like(center[..., :1])
    upper_side = jnp.concatenate([center[..., 1:], zero_plane], axis=4)
    lower_side = jnp.concatenate([zero_plane, center[..., :-1]], axis=4)
    flux_sum = (
        jnp.einsum("fg,gmxyz->fmxyz", jacobian[0], east_side - west_side, precision=highest)
        + jnp.einsum("fg,gmxyz->fmxyz", jacobian[1], north_side - south_side, precision=highest)
        + jnp.einsum("fg,gmxyz->fmxyz", jacobian[2], upper_side - lower_side, precision=highest)
    )
    source = wall_rows[:, :, :, None, :] * wall_line[None, None, None, :, None]
    neighbours = east_side + west_side + north_side + south_side + upper_side + lower_side
    return (
        -0.5 * flux_sum
        + NU_DAMP * (neighbours - 6.0 * center)
        - sponge_here[None, None] * center
        + source
    )


def gather_terms(node_piece, local_pos, weights):
    piece_size = node_piece.shape[1]
    inside = (local_pos >= 0) & (local_pos < piece_size)
    values_taken = jnp.take(node_piece, jnp.clip(local_pos, 0, piece_size - 1), axis=1)
    return jnp.sum(jnp.where(inside, weights, 0.0)[None] * values_taken, axis=1)


def face_rate(field_state, jacobian, sponge, wall_rows, wall_line):
    padded = padded_2(field_state, (("gx", 2), ("gy", 3)), 1)
    return rates(padded, jacobian, sponge, wall_rows, wall_line)


def runge_step(state, rate_fn, time_now):
    rate_one = rate_fn(state, time_now)
    rate_two = rate_fn(state + 0.5 * DT_STEP * rate_one, time_now + 0.5 * DT_STEP)
    rate_three = rate_fn(state + 0.5 * DT_STEP * rate_two, time_now + 0.5 * DT_STEP)
    rate_four = rate_fn(state + DT_STEP * rate_three, time_now + DT_STEP)
    return state + DT_STEP / 6.0 * (rate_one + 2.0 * rate_two + 2.0 * rate_three + rate_four)


def local(
    state_in, sponge, mean_velocity, wall_vector, mode_shapes, wall_nodes, wall_weights, wall_count
):
    modes_here = state_in.shape[1]
    cells_x = state_in.shape[2]
    cells_y = state_in.shape[3]
    cells_z = state_in.shape[4]
    gx_size = lax.axis_size("gx")
    gy_size = lax.axis_size("gy")
    gy_here = lax.axis_index("gy")
    jacobian = jacobians(mean_velocity)
    forcing = gather_terms(
        lax.all_gather(mode_shapes, ("gx", "gy"), axis=1, tiled=True), wall_nodes, wall_weights
    )
    wall_mask = (jnp.arange(cells_z)[None, :] < wall_count[:, None]).astype(jnp.float32)
    forcing = forcing * wall_mask[None]
    wall_rows = wall_vector[:, None, None, None] * forcing[None]
    state = state_in
    wall_base = (jnp.arange(cells_y) + gy_here * cells_y == 0).astype(jnp.float32)

    def advance(state_now, time_now):

        def rate_fn(field_state, time_at):
            return face_rate(field_state, jacobian, sponge, wall_rows, wall_base * pulse(time_at))

        return runge_step(state_now, rate_fn, time_now)

    stacked = []
    for step in range(STEPS):
        state = advance(state, step * DT_STEP)
        stacked.append(state)
    rows_total = 5.0 * cells_x * gx_size * cells_y * gy_size * cells_z
    snap_count = STEPS * modes_here
    snapshots = jnp.stack(stacked)
    local_gram = jnp.einsum(
        "sfmxyz,tfnxyz->smtn", snapshots, snapshots, precision=lax.Precision.HIGHEST
    ).reshape(snap_count, snap_count)
    gram_matrix = lax.psum(local_gram, ("gx", "gy")) / rows_total
    r_factor = jnp.linalg.cholesky(gram_matrix).T
    return (stacked[-1], r_factor)


def solution(mesh):
    placed = (
        P(None, None, "gx", "gy", None),
        P("gx", "gy", None),
        P(),
        P(),
        P(None, ("gx", "gy")),
        P(None, "gx", None),
        P(None, "gx", None),
        P("gx"),
    )
    return jax.shard_map(
        local,
        mesh=mesh,
        in_specs=placed,
        out_specs=(P(None, None, "gx", "gy", None), P()),
        check_vma=False,
    )
```

profile of v0, /device:TPU:0, one launch (start us, length us, event | category | flops | bytes accessed | tf_op | source)
XLA Modules:
  0.0 501.3 jit_solution(947815659723375712)
XLA Ops:
  5.2 6.3 %collective-permute-start.1 = (f32[5,16,1,8,128]{4,0,3,2,1:T(8,128)}, f32[5,16,1,8,128]{4,0,3,2,1:T(8,128)}, u32[]{:S(2)}, u32[]{:S(2)}) collective-permute-start(f32[5,16,1,8,128]{4,0,3,2,1:T(8,128)} %get-tuple-element.53), channel_id=1, source_target_pairs={{0,4},{4,8},{8,12},{12,16},{16,20},{20,24},{24,28},{1,5},{5,9},{9,... | collective-permute-start | bytes 983048 | tf_op jit(solution)/shard_map/ppermute | solution.py:23
  15.2 62.8 %all_gather.3 = f32[16,8192]{0,1:T(8,128)} all-gather(f32[16,256]{0,1:T(8,128)S(1)} %copy.42), channel_id=1, replica_groups=mesh['gx'=8,'gy'=4] {'gx','gy'}, dimensions={1}, use_global_device_ids=true | all-gather | bytes 540672 | tf_op jit(solution)/shard_map/all_gather | solution.py:102
  78.1 7.7 %gather_fusion = f32[2048,16]{1,0:T(8,128)S(1)} fusion(f32[16,8192]{0,1:T(8,128)} %all_gather.3, s32[2048]{0:T(1024)S(1)} %broadcast_clamp_fusion), kind=kCustom, calls=%fused_computation | custom fusion | bytes 270336 | tf_op jit(solution)/shard_map/jit(_take)/gather | solution.py:73
  87.3 6.4 %fusion.63 = f32[5,16,4,8,128]{4,0,3,2,1:T(8,128)} fusion(f32[5,16,4,8,127]{4,0,3,2,1:T(8,128)} %get-tuple-element.55, f32[5,16,4,8,127]{4,0,3,2,1:T(8,128)} %get-tuple-element.54, f32[5,5]{1,0:T(8,128)S(1)} %copy-done.5, f32[]{:T(128)} %bitcast.6), kind=kOutput, calls=%fused_computation.127 | convolution fusion | flops 19988556 | bytes 3911784 | tf_op jit(solution)/shard_map/fg,gmxyz->fmxyz/dot_general | solution.py:58
  112.0 8.1 %multiply_add_fusion.13 = (f32[5,16,4,8,128]{4,0,3,2,1:T(8,128)S(1)}, f32[5,16,4,8,128]{4,0,3,2,1:T(8,128)S(1)}) fusion(f32[5,16,4,8,128]{4,3,2,1,0:T(8,128)S(1)} %copy-done.3, f32[8]{0:T(128)S(1)} %broadcast_select_fusion.3, f32[5,16,4,128]{3,0,2,1:T(8,128)S(1)} %broadcast_multiply_fusion, f32[4,8,128]{2,1,0:T(8,128)S(1)} %copy-done.7, ...), kind=kOutput, calls=%fused_computation.124 | convolution fusion | flops 27852876 | bytes 13758600 | tf_op jit(solution)/shard_map/fg,gmxyz->fmxyz/dot_general | solution.py:56
  131.3 8.5 %collective-permute-done.4 = f32[5,16,1,8,128]{4,0,3,2,1:T(8,128)S(1)} collective-permute-done((f32[5,16,1,8,128]{4,0,3,2,1:T(8,128)S(1)}, f32[5,16,1,8,128]{4,0,3,2,1:T(8,128)S(1)}, u32[]{:S(2)}, u32[]{:S(2)}) %collective-permute-start.4) | collective-permute-done | bytes 327712 | tf_op jit(solution)/shard_map/ppermute | solution.py:24
  139.9 9.8 %collective-permute-start.7 = (f32[5,16,6,1,128]{4,0,3,2,1:T(8,128)S(1)}, f32[5,16,6,1,128]{4,0,3,2,1:T(8,128)S(1)}, u32[]{:S(2)}, u32[]{:S(2)}) collective-permute-start(f32[5,16,6,1,128]{4,0,3,2,1:T(8,128)S(1)} %get-tuple-element.20), channel_id=1, source_target_pairs={{0,1},{1,2},{2,3},{4,5},{5,6},{6,7},{8,9},{9,10},{10,11},{12,13},{... | collective-permute-start | bytes 737288 | tf_op jit(solution)/shard_map/ppermute | solution.py:23
  156.3 7.6 %multiply_add_fusion.12 = (f32[5,16,4,8,128]{4,0,3,2,1:T(8,128)S(1)}, f32[5,16,4,8,128]{4,0,3,2,1:T(8,128)}) fusion(f32[5,16,4,8,128]{4,3,2,1,0:T(8,128)S(1)} %copy-done.3, f32[8]{0:T(128)S(1)} %broadcast_select_fusion.2, f32[5,16,4,128]{3,0,2,1:T(8,128)S(1)} %broadcast_multiply_fusion, f32[5,16,4,8,128]{4,0,3,2,1:T(8,128)S(1)} %get-tuple-element.59, ...), kind=kOutput, calls=%fused_computation.117 | convolution fusion | flops 29163596 | bytes 11792520 | tf_op jit(solution)/shard_map/fg,gmxyz->fmxyz/dot_general | solution.py:56
  175.8 9.8 %collective-permute-done.8 = f32[5,16,1,8,128]{4,0,3,2,1:T(8,128)S(1)} collective-permute-done((f32[5,16,1,8,128]{4,0,3,2,1:T(8,128)S(1)}, f32[5,16,1,8,128]{4,0,3,2,1:T(8,128)S(1)}, u32[]{:S(2)}, u32[]{:S(2)}) %collective-permute-start.8) | collective-permute-done | bytes 327712 | tf_op jit(solution)/shard_map/ppermute | solution.py:24
  185.7 8.0 %collective-permute-start.11 = (f32[5,16,6,1,128]{4,0,3,2,1:T(8,128)S(1)}, f32[5,16,6,1,128]{4,0,3,2,1:T(8,128)S(1)}, u32[]{:S(2)}, u32[]{:S(2)}) collective-permute-start(f32[5,16,6,1,128]{4,0,3,2,1:T(8,128)S(1)} %get-tuple-element.18), channel_id=1, source_target_pairs={{0,1},{1,2},{2,3},{4,5},{5,6},{6,7},{8,9},{9,10},{10,11},{12,13},{... | collective-permute-start | bytes 737288 | tf_op jit(solution)/shard_map/ppermute | solution.py:23
  200.6 7.5 %multiply_add_fusion.11 = (f32[5,16,4,8,128]{4,0,3,2,1:T(8,128)S(1)}, f32[5,16,4,8,128]{4,0,3,2,1:T(8,128)}) fusion(f32[5,16,4,8,128]{4,3,2,1,0:T(8,128)S(1)} %copy-done.3, f32[8]{0:T(128)S(1)} %broadcast_select_fusion.2, f32[5,16,4,128]{3,0,2,1:T(8,128)S(1)} %broadcast_multiply_fusion, f32[5,16,4,8,128]{4,0,3,2,1:T(8,128)S(1)} %get-tuple-element.61, ...), kind=kOutput, calls=%fused_computation.110 | convolution fusion | flops 29163596 | bytes 11792520 | tf_op jit(solution)/shard_map/fg,gmxyz->fmxyz/dot_general | solution.py:56
  219.8 11.1 %collective-permute-done.12 = f32[5,16,1,8,128]{4,0,3,2,1:T(8,128)S(1)} collective-permute-done((f32[5,16,1,8,128]{4,0,3,2,1:T(8,128)S(1)}, f32[5,16,1,8,128]{4,0,3,2,1:T(8,128)S(1)}, u32[]{:S(2)}, u32[]{:S(2)}) %collective-permute-start.12) | collective-permute-done | bytes 327712 | tf_op jit(solution)/shard_map/ppermute | solution.py:24
  244.4 8.5 %fusion.6 = f32[5,16,4,8,128]{4,0,3,2,1:T(8,128)S(1)} fusion(f32[5,16,4,8,128]{4,0,3,2,1:T(8,128)S(1)} %get-tuple-element.63, f32[5,16,4,8,128]{4,0,3,2,1:T(8,128)S(1)} %fusion.39, f32[5,16,4,8,128]{4,0,3,2,1:T(8,128)S(1)} %fusion.41, f32[5,16,1,8,128]{4,0,3,2,1:T(8,128)S(1)} %collective-permute-done.12, ...), kind=kOutput, calls=%fused_computation.14 | convolution fusion | flops 32112716 | bytes 14413992 | tf_op jit(solution)/shard_map/fg,gmxyz->fmxyz/dot_general | solution.py:56
  264.7 12.4 %collective-permute-done.16 = f32[5,16,1,8,128]{4,0,3,2,1:T(8,128)S(1)} collective-permute-done((f32[5,16,1,8,128]{4,0,3,2,1:T(8,128)S(1)}, f32[5,16,1,8,128]{4,0,3,2,1:T(8,128)S(1)}, u32[]{:S(2)}, u32[]{:S(2)}) %collective-permute-start.16) | collective-permute-done | bytes 327712 | tf_op jit(solution)/shard_map/ppermute | solution.py:24
  277.1 6.2 %collective-permute-start.19 = (f32[5,16,6,1,128]{4,0,3,2,1:T(8,128)S(1)}, f32[5,16,6,1,128]{4,0,3,2,1:T(8,128)S(1)}, u32[]{:S(2)}, u32[]{:S(2)}) collective-permute-start(f32[5,16,6,1,128]{4,0,3,2,1:T(8,128)S(1)} %get-tuple-element.14), channel_id=1, source_target_pairs={{0,1},{1,2},{2,3},{4,5},{5,6},{6,7},{8,9},{9,10},{10,11},{12,13},{... | collective-permute-start | bytes 737288 | tf_op jit(solution)/shard_map/ppermute | solution.py:23
  309.2 11.8 %collective-permute-done.20 = f32[5,16,1,8,128]{4,0,3,2,1:T(8,128)S(1)} collective-permute-done((f32[5,16,1,8,128]{4,0,3,2,1:T(8,128)S(1)}, f32[5,16,1,8,128]{4,0,3,2,1:T(8,128)S(1)}, u32[]{:S(2)}, u32[]{:S(2)}) %collective-permute-start.20) | collective-permute-done | bytes 327712 | tf_op jit(solution)/shard_map/ppermute | solution.py:24
  321.0 6.3 %collective-permute-start.23 = (f32[5,16,6,1,128]{4,0,3,2,1:T(8,128)S(1)}, f32[5,16,6,1,128]{4,0,3,2,1:T(8,128)S(1)}, u32[]{:S(2)}, u32[]{:S(2)}) collective-permute-start(f32[5,16,6,1,128]{4,0,3,2,1:T(8,128)S(1)} %get-tuple-element.12), channel_id=1, source_target_pairs={{0,1},{1,2},{2,3},{4,5},{5,6},{6,7},{8,9},{9,10},{10,11},{12,13},{... | collective-permute-start | bytes 737288 | tf_op jit(solution)/shard_map/ppermute | solution.py:23
  351.7 11.8 %collective-permute-done.24 = f32[5,16,1,8,128]{4,0,3,2,1:T(8,128)S(1)} collective-permute-done((f32[5,16,1,8,128]{4,0,3,2,1:T(8,128)S(1)}, f32[5,16,1,8,128]{4,0,3,2,1:T(8,128)S(1)}, u32[]{:S(2)}, u32[]{:S(2)}) %collective-permute-start.24) | collective-permute-done | bytes 327712 | tf_op jit(solution)/shard_map/ppermute | solution.py:24
  363.6 6.3 %collective-permute-start.27 = (f32[5,16,6,1,128]{4,0,3,2,1:T(8,128)S(1)}, f32[5,16,6,1,128]{4,0,3,2,1:T(8,128)S(1)}, u32[]{:S(2)}, u32[]{:S(2)}) collective-permute-start(f32[5,16,6,1,128]{4,0,3,2,1:T(8,128)S(1)} %get-tuple-element.10), channel_id=1, source_target_pairs={{0,1},{1,2},{2,3},{4,5},{5,6},{6,7},{8,9},{9,10},{10,11},{12,13},{... | collective-permute-start | bytes 737288 | tf_op jit(solution)/shard_map/ppermute | solution.py:23
  395.3 11.8 %collective-permute-done.28 = f32[5,16,1,8,128]{4,0,3,2,1:T(8,128)S(1)} collective-permute-done((f32[5,16,1,8,128]{4,0,3,2,1:T(8,128)S(1)}, f32[5,16,1,8,128]{4,0,3,2,1:T(8,128)S(1)}, u32[]{:S(2)}, u32[]{:S(2)}) %collective-permute-start.28) | collective-permute-done | bytes 327712 | tf_op jit(solution)/shard_map/ppermute | solution.py:24
  407.2 6.7 %collective-permute-start.31 = (f32[5,16,6,1,128]{4,0,3,2,1:T(8,128)S(1)}, f32[5,16,6,1,128]{4,0,3,2,1:T(8,128)S(1)}, u32[]{:S(2)}, u32[]{:S(2)}) collective-permute-start(f32[5,16,6,1,128]{4,0,3,2,1:T(8,128)S(1)} %get-tuple-element.8), channel_id=1, source_target_pairs={{0,1},{1,2},{2,3},{4,5},{5,6},{6,7},{8,9},{9,10},{10,11},{12,13},{... | collective-permute-start | bytes 737288 | tf_op jit(solution)/shard_map/ppermute | solution.py:23
  422.3 7.5 %multiply_add_fusion.6 = f32[5,16,4,8,128]{4,0,3,2,1:T(8,128)S(1)} fusion(f32[5,16,4,8,128]{4,0,3,2,1:T(8,128)S(1)} %fusion.6, f32[5,16,4,8,128]{4,0,3,2,1:T(8,128)S(1)} %get-tuple-element.69, f32[5,16,4,8,128]{4,0,3,2,1:T(8,128)S(1)} %fusion.7, f32[5,16,4,8,128]{4,0,3,2,1:T(8,128)} %fusion.9, f32[5,16,1,8,128]{4,0,3,2,1:T(8,128)S(1)} %collective-permute-done.28, ...), kind=kOutput, calls=%fused_computation.75 | convolution fusion | flops 32112716 | bytes 14413992 | tf_op jit(solution)/shard_map/fg,gmxyz->fmxyz/dot_general | solution.py:56
  432.2 11.1 %fusion.87 = f32[2,16,2,16]{3,1,2,0:T(8,128)S(1)} fusion(f32[2,5,16,4,8,128]{5,1,4,3,2,0:T(8,128)S(1)} %get-tuple-element.7, f32[2,5,16,4,8,128,1]{5,1,4,3,2,0,6:T(8,128)S(1)} %get-tuple-element.6), kind=kOutput, calls=%fused_computation.150 | convolution fusion | flops 251658240 | bytes 5246976 | tf_op jit(solution)/shard_map/sfmxyz,tfnxyz->smtn/dot_general | solution.py:124
  443.5 52.5 %psum.7 = f32[32,32]{0,1:T(8,128)S(1)} all-reduce(f32[32,32]{0,1:T(8,128)S(1)} %reshape.62), channel_id=1, replica_groups=mesh['gx'=8,'gy'=4] {'gx','gy'}, use_global_device_ids=true, to_apply=%region_1.2 | all-reduce | flops 1024 | bytes 8192 | tf_op jit(solution)/shard_map/psum | solution.py:127
  (154 shorter events, 193.1 us)
Async XLA Ops:
  3.9 91.8 %collective-permute-start = (f32[5,16,1,8,128]{4,0,3,2,1:T(8,128)}, f32[5,16,1,8,128]{4,0,3,2,1:T(8,128)}, u32[]{:S(2)}, u32[]{:S(2)}) collective-permute-start(f32[5,16,1,8,128]{4,0,3,2,1:T(8,128)} %get-tuple-element.52), channel_id=1, source_target_pairs={{4,0},{8,4},{12,8},{16,12},{20,16},{24,20},{28,24},{5,1},{9,5},{13... | collective-permute-start | bytes 983048 | tf_op jit(solution)/shard_map/ppermute | solution.py:24
  5.2 88.5 %collective-permute-start.1 = (f32[5,16,1,8,128]{4,0,3,2,1:T(8,128)}, f32[5,16,1,8,128]{4,0,3,2,1:T(8,128)}, u32[]{:S(2)}, u32[]{:S(2)}) collective-permute-start(f32[5,16,1,8,128]{4,0,3,2,1:T(8,128)} %get-tuple-element.53), channel_id=1, source_target_pairs={{0,4},{4,8},{8,12},{12,16},{16,20},{20,24},{24,28},{1,5},{5,9},{9,... | collective-permute-start | bytes 983048 | tf_op jit(solution)/shard_map/ppermute | solution.py:23
  99.5 5.5 %collective-permute-start.3 = (f32[5,16,6,1,128]{4,0,3,2,1:T(8,128)}, f32[5,16,6,1,128]{4,0,3,2,1:T(8,128)}, u32[]{:S(2)}, u32[]{:S(2)}) collective-permute-start(f32[5,16,6,1,128]{4,0,3,2,1:T(8,128)} %get-tuple-element.22), channel_id=1, source_target_pairs={{0,1},{1,2},{2,3},{4,5},{5,6},{6,7},{8,9},{9,10},{10,11},{12,13},{... | collective-permute-start | bytes 737288 | tf_op jit(solution)/shard_map/ppermute | solution.py:23
  120.2 11.0 %collective-permute-start.5 = (f32[5,16,1,8,128]{4,0,3,2,1:T(8,128)S(1)}, f32[5,16,1,8,128]{4,0,3,2,1:T(8,128)S(1)}, u32[]{:S(2)}, u32[]{:S(2)}) collective-permute-start(f32[5,16,1,8,128]{4,0,3,2,1:T(8,128)S(1)} %get-tuple-element.48), channel_id=1, source_target_pairs={{0,4},{4,8},{8,12},{12,16},{16,20},{20,24},{24,28},{1,5},{5,9},{9,... | collective-permute-start | bytes 983048 | tf_op jit(solution)/shard_map/ppermute | solution.py:23
  124.1 15.7 %collective-permute-start.4 = (f32[5,16,1,8,128]{4,0,3,2,1:T(8,128)S(1)}, f32[5,16,1,8,128]{4,0,3,2,1:T(8,128)S(1)}, u32[]{:S(2)}, u32[]{:S(2)}) collective-permute-start(f32[5,16,1,8,128]{4,0,3,2,1:T(8,128)S(1)} %get-tuple-element.49), channel_id=1, source_target_pairs={{4,0},{8,4},{12,8},{16,12},{20,16},{24,20},{28,24},{5,1},{9,5},{13... | collective-permute-start | bytes 983048 | tf_op jit(solution)/shard_map/ppermute | solution.py:24
  139.9 14.0 %collective-permute-start.7 = (f32[5,16,6,1,128]{4,0,3,2,1:T(8,128)S(1)}, f32[5,16,6,1,128]{4,0,3,2,1:T(8,128)S(1)}, u32[]{:S(2)}, u32[]{:S(2)}) collective-permute-start(f32[5,16,6,1,128]{4,0,3,2,1:T(8,128)S(1)} %get-tuple-element.20), channel_id=1, source_target_pairs={{0,1},{1,2},{2,3},{4,5},{5,6},{6,7},{8,9},{9,10},{10,11},{12,13},{... | collective-permute-start | bytes 737288 | tf_op jit(solution)/shard_map/ppermute | solution.py:23
  164.0 11.8 %collective-permute-start.9 = (f32[5,16,1,8,128]{4,0,3,2,1:T(8,128)S(1)}, f32[5,16,1,8,128]{4,0,3,2,1:T(8,128)S(1)}, u32[]{:S(2)}, u32[]{:S(2)}) collective-permute-start(f32[5,16,1,8,128]{4,0,3,2,1:T(8,128)S(1)} %get-tuple-element.44), channel_id=1, source_target_pairs={{0,4},{4,8},{8,12},{12,16},{16,20},{20,24},{24,28},{1,5},{5,9},{9,... | collective-permute-start | bytes 983048 | tf_op jit(solution)/shard_map/ppermute | solution.py:23
  168.1 17.5 %collective-permute-start.8 = (f32[5,16,1,8,128]{4,0,3,2,1:T(8,128)S(1)}, f32[5,16,1,8,128]{4,0,3,2,1:T(8,128)S(1)}, u32[]{:S(2)}, u32[]{:S(2)}) collective-permute-start(f32[5,16,1,8,128]{4,0,3,2,1:T(8,128)S(1)} %get-tuple-element.45), channel_id=1, source_target_pairs={{4,0},{8,4},{12,8},{16,12},{20,16},{24,20},{28,24},{5,1},{9,5},{13... | collective-permute-start | bytes 983048 | tf_op jit(solution)/shard_map/ppermute | solution.py:24
  185.7 12.4 %collective-permute-start.11 = (f32[5,16,6,1,128]{4,0,3,2,1:T(8,128)S(1)}, f32[5,16,6,1,128]{4,0,3,2,1:T(8,128)S(1)}, u32[]{:S(2)}, u32[]{:S(2)}) collective-permute-start(f32[5,16,6,1,128]{4,0,3,2,1:T(8,128)S(1)} %get-tuple-element.18), channel_id=1, source_target_pairs={{0,1},{1,2},{2,3},{4,5},{5,6},{6,7},{8,9},{9,10},{10,11},{12,13},{... | collective-permute-start | bytes 737288 | tf_op jit(solution)/shard_map/ppermute | solution.py:23
  208.1 11.7 %collective-permute-start.13 = (f32[5,16,1,8,128]{4,0,3,2,1:T(8,128)S(1)}, f32[5,16,1,8,128]{4,0,3,2,1:T(8,128)S(1)}, u32[]{:S(2)}, u32[]{:S(2)}) collective-permute-start(f32[5,16,1,8,128]{4,0,3,2,1:T(8,128)S(1)} %get-tuple-element.40), channel_id=1, source_target_pairs={{0,4},{4,8},{8,12},{12,16},{16,20},{20,24},{24,28},{1,5},{5,9},{9,... | collective-permute-start | bytes 983048 | tf_op jit(solution)/shard_map/ppermute | solution.py:23
  212.2 18.6 %collective-permute-start.12 = (f32[5,16,1,8,128]{4,0,3,2,1:T(8,128)S(1)}, f32[5,16,1,8,128]{4,0,3,2,1:T(8,128)S(1)}, u32[]{:S(2)}, u32[]{:S(2)}) collective-permute-start(f32[5,16,1,8,128]{4,0,3,2,1:T(8,128)S(1)} %get-tuple-element.41), channel_id=1, source_target_pairs={{4,0},{8,4},{12,8},{16,12},{20,16},{24,20},{28,24},{5,1},{9,5},{13... | collective-permute-start | bytes 983048 | tf_op jit(solution)/shard_map/ppermute | solution.py:24
  230.9 10.5 %collective-permute-start.15 = (f32[5,16,6,1,128]{4,0,3,2,1:T(8,128)S(1)}, f32[5,16,6,1,128]{4,0,3,2,1:T(8,128)S(1)}, u32[]{:S(2)}, u32[]{:S(2)}) collective-permute-start(f32[5,16,6,1,128]{4,0,3,2,1:T(8,128)S(1)} %get-tuple-element.16), channel_id=1, source_target_pairs={{0,1},{1,2},{2,3},{4,5},{5,6},{6,7},{8,9},{9,10},{10,11},{12,13},{... | collective-permute-start | bytes 737288 | tf_op jit(solution)/shard_map/ppermute | solution.py:23
  253.0 11.7 %collective-permute-start.17 = (f32[5,16,1,8,128]{4,0,3,2,1:T(8,128)S(1)}, f32[5,16,1,8,128]{4,0,3,2,1:T(8,128)S(1)}, u32[]{:S(2)}, u32[]{:S(2)}) collective-permute-start(f32[5,16,1,8,128]{4,0,3,2,1:T(8,128)S(1)} %get-tuple-element.36), channel_id=1, source_target_pairs={{0,4},{4,8},{8,12},{12,16},{16,20},{20,24},{24,28},{1,5},{5,9},{9,... | collective-permute-start | bytes 983048 | tf_op jit(solution)/shard_map/ppermute | solution.py:23
  257.4 19.6 %collective-permute-start.16 = (f32[5,16,1,8,128]{4,0,3,2,1:T(8,128)S(1)}, f32[5,16,1,8,128]{4,0,3,2,1:T(8,128)S(1)}, u32[]{:S(2)}, u32[]{:S(2)}) collective-permute-start(f32[5,16,1,8,128]{4,0,3,2,1:T(8,128)S(1)} %get-tuple-element.37), channel_id=1, source_target_pairs={{4,0},{8,4},{12,8},{16,12},{20,16},{24,20},{28,24},{5,1},{9,5},{13... | collective-permute-start | bytes 983048 | tf_op jit(solution)/shard_map/ppermute | solution.py:24
  277.1 10.7 %collective-permute-start.19 = (f32[5,16,6,1,128]{4,0,3,2,1:T(8,128)S(1)}, f32[5,16,6,1,128]{4,0,3,2,1:T(8,128)S(1)}, u32[]{:S(2)}, u32[]{:S(2)}) collective-permute-start(f32[5,16,6,1,128]{4,0,3,2,1:T(8,128)S(1)} %get-tuple-element.14), channel_id=1, source_target_pairs={{0,1},{1,2},{2,3},{4,5},{5,6},{6,7},{8,9},{9,10},{10,11},{12,13},{... | collective-permute-start | bytes 737288 | tf_op jit(solution)/shard_map/ppermute | solution.py:23
  296.5 12.7 %collective-permute-start.21 = (f32[5,16,1,8,128]{4,0,3,2,1:T(8,128)S(1)}, f32[5,16,1,8,128]{4,0,3,2,1:T(8,128)S(1)}, u32[]{:S(2)}, u32[]{:S(2)}) collective-permute-start(f32[5,16,1,8,128]{4,0,3,2,1:T(8,128)S(1)} %get-tuple-element.32), channel_id=1, source_target_pairs={{0,4},{4,8},{8,12},{12,16},{16,20},{20,24},{24,28},{1,5},{5,9},{9,... | collective-permute-start | bytes 983048 | tf_op jit(solution)/shard_map/ppermute | solution.py:23
  301.3 19.6 %collective-permute-start.20 = (f32[5,16,1,8,128]{4,0,3,2,1:T(8,128)S(1)}, f32[5,16,1,8,128]{4,0,3,2,1:T(8,128)S(1)}, u32[]{:S(2)}, u32[]{:S(2)}) collective-permute-start(f32[5,16,1,8,128]{4,0,3,2,1:T(8,128)S(1)} %get-tuple-element.33), channel_id=1, source_target_pairs={{4,0},{8,4},{12,8},{16,12},{20,16},{24,20},{28,24},{5,1},{9,5},{13... | collective-permute-start | bytes 983048 | tf_op jit(solution)/shard_map/ppermute | solution.py:24
  321.0 10.9 %collective-permute-start.23 = (f32[5,16,6,1,128]{4,0,3,2,1:T(8,128)S(1)}, f32[5,16,6,1,128]{4,0,3,2,1:T(8,128)S(1)}, u32[]{:S(2)}, u32[]{:S(2)}) collective-permute-start(f32[5,16,6,1,128]{4,0,3,2,1:T(8,128)S(1)} %get-tuple-element.12), channel_id=1, source_target_pairs={{0,1},{1,2},{2,3},{4,5},{5,6},{6,7},{8,9},{9,10},{10,11},{12,13},{... | collective-permute-start | bytes 737288 | tf_op jit(solution)/shard_map/ppermute | solution.py:23
  339.0 12.7 %collective-permute-start.25 = (f32[5,16,1,8,128]{4,0,3,2,1:T(8,128)S(1)}, f32[5,16,1,8,128]{4,0,3,2,1:T(8,128)S(1)}, u32[]{:S(2)}, u32[]{:S(2)}) collective-permute-start(f32[5,16,1,8,128]{4,0,3,2,1:T(8,128)S(1)} %get-tuple-element.28), channel_id=1, source_target_pairs={{0,4},{4,8},{8,12},{12,16},{16,20},{20,24},{24,28},{1,5},{5,9},{9,... | collective-permute-start | bytes 983048 | tf_op jit(solution)/shard_map/ppermute | solution.py:23
  343.9 19.6 %collective-permute-start.24 = (f32[5,16,1,8,128]{4,0,3,2,1:T(8,128)S(1)}, f32[5,16,1,8,128]{4,0,3,2,1:T(8,128)S(1)}, u32[]{:S(2)}, u32[]{:S(2)}) collective-permute-start(f32[5,16,1,8,128]{4,0,3,2,1:T(8,128)S(1)} %get-tuple-element.29), channel_id=1, source_target_pairs={{4,0},{8,4},{12,8},{16,12},{20,16},{24,20},{28,24},{5,1},{9,5},{13... | collective-permute-start | bytes 983048 | tf_op jit(solution)/shard_map/ppermute | solution.py:24
  363.6 10.7 %collective-permute-start.27 = (f32[5,16,6,1,128]{4,0,3,2,1:T(8,128)S(1)}, f32[5,16,6,1,128]{4,0,3,2,1:T(8,128)S(1)}, u32[]{:S(2)}, u32[]{:S(2)}) collective-permute-start(f32[5,16,6,1,128]{4,0,3,2,1:T(8,128)S(1)} %get-tuple-element.10), channel_id=1, source_target_pairs={{0,1},{1,2},{2,3},{4,5},{5,6},{6,7},{8,9},{9,10},{10,11},{12,13},{... | collective-permute-start | bytes 737288 | tf_op jit(solution)/shard_map/ppermute | solution.py:23
  383.1 12.3 %collective-permute-start.29 = (f32[5,16,1,8,128]{4,0,3,2,1:T(8,128)S(1)}, f32[5,16,1,8,128]{4,0,3,2,1:T(8,128)S(1)}, u32[]{:S(2)}, u32[]{:S(2)}) collective-permute-start(f32[5,16,1,8,128]{4,0,3,2,1:T(8,128)S(1)} %get-tuple-element.24), channel_id=1, source_target_pairs={{0,4},{4,8},{8,12},{12,16},{16,20},{20,24},{24,28},{1,5},{5,9},{9,... | collective-permute-start | bytes 983048 | tf_op jit(solution)/shard_map/ppermute | solution.py:23
  387.9 19.3 %collective-permute-start.28 = (f32[5,16,1,8,128]{4,0,3,2,1:T(8,128)S(1)}, f32[5,16,1,8,128]{4,0,3,2,1:T(8,128)S(1)}, u32[]{:S(2)}, u32[]{:S(2)}) collective-permute-start(f32[5,16,1,8,128]{4,0,3,2,1:T(8,128)S(1)} %get-tuple-element.25), channel_id=1, source_target_pairs={{4,0},{8,4},{12,8},{16,12},{20,16},{24,20},{28,24},{5,1},{9,5},{13... | collective-permute-start | bytes 983048 | tf_op jit(solution)/shard_map/ppermute | solution.py:24
  407.2 10.8 %collective-permute-start.31 = (f32[5,16,6,1,128]{4,0,3,2,1:T(8,128)S(1)}, f32[5,16,6,1,128]{4,0,3,2,1:T(8,128)S(1)}, u32[]{:S(2)}, u32[]{:S(2)}) collective-permute-start(f32[5,16,6,1,128]{4,0,3,2,1:T(8,128)S(1)} %get-tuple-element.8), channel_id=1, source_target_pairs={{0,1},{1,2},{2,3},{4,5},{5,6},{6,7},{8,9},{9,10},{10,11},{12,13},{... | collective-permute-start | bytes 737288 | tf_op jit(solution)/shard_map/ppermute | solution.py:23
  (23 other events, 126.8 us)
where the time goes:
time: 511 us; the launch traced here: 501 us
  matrix products  117 us (23%)
  waiting for transfers between devices  117 us (23%)
  blocking collectives  115 us (23%)
  starting transfers between devices  112 us (22%)
  local copies, waits for them, and re-layouts  29.7 us (6%)
  other arithmetic  7.58 us (1%)
    ppermute x16, starting transfers between devices, padded_2(): before = lax.ppermute(last, axis, up)  89.7 us
    ppermute x16, waiting for transfers between devices, padded_2(): after = lax.ppermute(initial, axis, down)  79.9 us
    all_gather x1, blocking collectives, local(): lax.all_gather(mode_shapes, ('gx', 'gy'), axis=1, tiled=True)  62.8 us
    dot_general x8, matrix products, rates(): jnp.einsum('fg,gmxyz->fmxyz', jacobian[0], east_side - west_side, precisi...  55.9 us
    psum x1, blocking collectives, local(): gram_matrix = lax.psum(local_gram, ('gx', 'gy')) / rows_total  52.5 us
    ppermute x16, waiting for transfers between devices, padded_2(): before = lax.ppermute(last, axis, up)  37.6 us
    dot_general x8, matrix products, rates(): jnp.einsum('fg,gmxyz->fmxyz', jacobian[2], upper_side - lower_side, preci...  26.5 us
    dot_general x8, matrix products, rates(): jnp.einsum('fg,gmxyz->fmxyz', jacobian[1], north_side - south_side, preci...  23.8 us
  transfers between devices with their start and end apart: 32, of which 17 were waited for; matrix products, arithmetic and copies ran while one was open for 10% of the time, Pallas kernels for 0%

commit v1 on v0

--- a/solution.py
+++ b/solution.py
@@ -11,6 +11,34 @@
 DT_STEP = 0.4
 PULSE_MID = 0.8
 PULSE_WIDTH = 0.5
+
+
+def positions_answer(here_x, d_out):
+    here_x = jnp.moveaxis(here_x, 0, d_out)
+    block_now = here_x.shape
+    s_next = here_x.reshape(
+        *block_now[:d_out], block_now[d_out] * block_now[d_out + 1], *block_now[d_out + 2 :]
+    )
+    return s_next
+
+
+def manage_streams_now(u, mesh_dim):
+    dev_count = lax.axis_size(mesh_dim)
+    state_next = u[None]
+    for kk in range(dev_count.bit_length() - 1):
+        kept_arr = 1 << kk
+        later = lax.ppermute(
+            state_next, mesh_dim, perm=list(map(lambda m: (m, m ^ kept_arr), range(dev_count)))
+        )
+        outer = jnp.stack([state_next, later], axis=0)
+        view_out = lax.axis_index(mesh_dim) >> kk & 1
+        state_next = jnp.where(view_out == 0, outer, outer[::-1]).reshape(-1, *u.shape)
+    return state_next
+
+
+def _guide_pairs_all(vals, out_dim, piece_in):
+    block_last = positions_answer(manage_streams_now(piece_in, vals), out_dim)
+    return block_last
 
 
 def padded_2(x, sides, width):
@@ -99,7 +127,7 @@
     gy_here = lax.axis_index("gy")
     jacobian = jacobians(mean_velocity)
     forcing = gather_terms(
-        lax.all_gather(mode_shapes, ("gx", "gy"), axis=1, tiled=True), wall_nodes, wall_weights
+        _guide_pairs_all(("gx", "gy"), 1, piece_in=mode_shapes), wall_nodes, wall_weights
     )
     wall_mask = (jnp.arange(cells_z)[None, :] < wall_count[:, None]).astype(jnp.float32)
     forcing = forcing * wall_mask[None]

time: 511 us -> 470 us (0.920)
  blocking collectives: 115 us -> 49.3 us
  starting transfers between devices: 112 us -> 132 us
  other arithmetic: 7.58 us -> 14.5 us
  local copies, waits for them, and re-layouts: 29.7 us -> 35.3 us
    all_gather x1 -> x0, blocking collectives: 62.8 us -> none  [local(): lax.all_gather(mode_shapes, ('gx', 'gy'), axis=1, tiled=True)]
    ppermute x16, waiting for transfers between devices: 79.9 us -> 28.4 us  [padded_2(): after = lax.ppermute(initial, axis, down)]
    ppermute x16, waiting for transfers between devices: 37.6 us -> 73.9 us  [padded_2(): before = lax.ppermute(last, axis, up)]
    ppermute x0 -> x5, waiting for transfers between devices: none -> 10.7 us  [manage_streams_now(): lax.ppermute(state_next, mesh_dim, perm=list(map(lambda m: (m, m ^ kept_a...]
    ppermute x16, starting transfers between devices: 89.7 us -> 100 us  [padded_2(): before = lax.ppermute(last, axis, up)]
    ppermute x0 -> x5, starting transfers between devices: none -> 9.07 us  [manage_streams_now(): lax.ppermute(state_next, mesh_dim, perm=list(map(lambda m: (m, m ^ kept_a...]
  transfers between devices with their start and end apart: 32 -> 37, of which waited for: 17 -> 19; matrix products, arithmetic and copies ran while one was open for 10% -> 14% of each run, Pallas kernels for 0% -> 0%
where the time goes in v1:
time: 470 us; the launch traced here: 463 us
  starting transfers between devices  132 us (28%)
  matrix products  117 us (25%)
  waiting for transfers between devices  113 us (24%)
  blocking collectives  49.3 us (10%)
  local copies, waits for them, and re-layouts  35.3 us (8%)
  other arithmetic  14.5 us (3%)
    ppermute x16, starting transfers between devices, padded_2(): before = lax.ppermute(last, axis, up)  100 us
    ppermute x16, waiting for transfers between devices, padded_2(): before = lax.ppermute(last, axis, up)  73.9 us
    dot_general x8, matrix products, rates(): jnp.einsum('fg,gmxyz->fmxyz', jacobian[0], east_side - west_side, precisi...  55.8 us
    psum x1, blocking collectives, local(): gram_matrix = lax.psum(local_gram, ('gx', 'gy')) / rows_total  49.3 us
    ppermute x16, waiting for transfers between devices, padded_2(): after = lax.ppermute(initial, axis, down)  28.4 us
    dot_general x8, matrix products, rates(): jnp.einsum('fg,gmxyz->fmxyz', jacobian[2], upper_side - lower_side, preci...  25.9 us
    dot_general x8, matrix products, rates(): jnp.einsum('fg,gmxyz->fmxyz', jacobian[1], north_side - south_side, preci...  24.5 us
    ppermute x16, starting transfers between devices, padded_2(): after = lax.ppermute(initial, axis, down)  22.7 us
  transfers between devices with their start and end apart: 37, of which 19 were waited for; matrix products, arithmetic and copies ran while one was open for 14% of the time, Pallas kernels for 0%

profile of v1, /device:TPU:0, one launch (start us, length us, event | category | flops | bytes accessed | tf_op | source)
XLA Modules:
  0.0 463.3 jit_solution(790995847828036709)
XLA Ops:
  5.7 5.9 %collective-permute-start.1 = (f32[5,16,1,8,128]{4,0,3,2,1:T(8,128)}, f32[5,16,1,8,128]{4,0,3,2,1:T(8,128)}, u32[]{:S(2)}, u32[]{:S(2)}) collective-permute-start(f32[5,16,1,8,128]{4,0,3,2,1:T(8,128)} %get-tuple-element.53), channel_id=1, source_target_pairs={{0,4},{4,8},{8,12},{12,16},{16,20},{20,24},{24,28},{1,5},{5,9},{9,... | collective-permute-start | bytes 983048 | tf_op jit(solution)/shard_map/ppermute | solution.py:51
  16.3 6.3 %fusion.63 = f32[5,16,4,8,128]{4,0,3,2,1:T(8,128)} fusion(f32[5,16,4,8,127]{4,0,3,2,1:T(8,128)} %get-tuple-element.55, f32[5,16,4,8,127]{4,0,3,2,1:T(8,128)} %get-tuple-element.54, f32[5,5]{1,0:T(8,128)S(1)} %copy-done.5, f32[]{:T(128)} %bitcast.6), kind=kOutput, calls=%fused_computation.127 | convolution fusion | flops 19988556 | bytes 3911784 | tf_op jit(solution)/shard_map/fg,gmxyz->fmxyz/dot_general | solution.py:86
  59.5 9.8 %gather_fusion = f32[2048,16]{1,0:T(8,128)} fusion(f32[16,8192]{0,1:T(8,128)} %bitcast.120, s32[2048]{0:T(1024)S(1)} %copy-done.7), kind=kCustom, calls=%fused_computation | custom fusion | bytes 270336 | tf_op jit(solution)/shard_map/jit(_take)/gather | solution.py:101
  78.7 8.2 %multiply_add_fusion.13 = (f32[5,16,4,8,128]{4,0,3,2,1:T(8,128)S(1)}, f32[5,16,4,8,128]{4,0,3,2,1:T(8,128)S(1)}) fusion(f32[5,16,4,8,128]{4,3,2,1,0:T(8,128)S(1)} %copy-done.3, f32[8]{0:T(128)S(1)} %copy-done.15, f32[5,16,4,128]{3,0,2,1:T(8,128)S(1)} %broadcast_multiply_fusion, f32[4,8,128]{2,1,0:T(8,128)S(1)} %copy-done.8, ...), kind=kOutput, calls=%fused_computation.124 | convolution fusion | flops 27852876 | bytes 13758600 | tf_op jit(solution)/shard_map/fg,gmxyz->fmxyz/dot_general | solution.py:84
  93.5 20.5 %collective-permute-done.10 = f32[5,16,1,8,128]{4,0,3,2,1:T(8,128)S(1)} collective-permute-done((f32[5,16,1,8,128]{4,0,3,2,1:T(8,128)S(1)}, f32[5,16,1,8,128]{4,0,3,2,1:T(8,128)S(1)}, u32[]{:S(2)}, u32[]{:S(2)}) %collective-permute-start.10) | collective-permute-done | bytes 327712 | tf_op jit(solution)/shard_map/ppermute | solution.py:51
  122.9 7.5 %multiply_add_fusion.12 = (f32[5,16,4,8,128]{4,0,3,2,1:T(8,128)S(1)}, f32[5,16,4,8,128]{4,0,3,2,1:T(8,128)}) fusion(f32[5,16,4,8,128]{4,3,2,1,0:T(8,128)S(1)} %copy-done.3, f32[8]{0:T(128)S(1)} %copy-done.21, f32[5,16,4,128]{3,0,2,1:T(8,128)S(1)} %broadcast_multiply_fusion, f32[5,16,4,8,128]{4,0,3,2,1:T(8,128)S(1)} %get-tuple-element.61, ...), kind=kOutput, calls=%fused_computation.117 | convolution fusion | flops 29163596 | bytes 11792520 | tf_op jit(solution)/shard_map/fg,gmxyz->fmxyz/dot_general | solution.py:84
  137.1 16.9 %collective-permute-done.14 = f32[5,16,1,8,128]{4,0,3,2,1:T(8,128)S(1)} collective-permute-done((f32[5,16,1,8,128]{4,0,3,2,1:T(8,128)S(1)}, f32[5,16,1,8,128]{4,0,3,2,1:T(8,128)S(1)}, u32[]{:S(2)}, u32[]{:S(2)}) %collective-permute-start.14) | collective-permute-done | bytes 327712 | tf_op jit(solution)/shard_map/ppermute | solution.py:51
  154.0 6.5 %collective-permute-start.16 = (f32[5,16,6,1,128]{4,0,3,2,1:T(8,128)S(1)}, f32[5,16,6,1,128]{4,0,3,2,1:T(8,128)S(1)}, u32[]{:S(2)}, u32[]{:S(2)}) collective-permute-start(f32[5,16,6,1,128]{4,0,3,2,1:T(8,128)S(1)} %get-tuple-element.18), channel_id=1, source_target_pairs={{0,1},{1,2},{2,3},{4,5},{5,6},{6,7},{8,9},{9,10},{10,11},{12,13},{... | collective-permute-start | bytes 737288 | tf_op jit(solution)/shard_map/ppermute | solution.py:51
  167.8 7.4 %multiply_add_fusion.11 = (f32[5,16,4,8,128]{4,0,3,2,1:T(8,128)S(1)}, f32[5,16,4,8,128]{4,0,3,2,1:T(8,128)}) fusion(f32[5,16,4,8,128]{4,3,2,1,0:T(8,128)S(1)} %copy-done.3, f32[8]{0:T(128)S(1)} %copy-done.21, f32[5,16,4,128]{3,0,2,1:T(8,128)S(1)} %broadcast_multiply_fusion, f32[5,16,4,8,128]{4,0,3,2,1:T(8,128)S(1)} %get-tuple-element.63, ...), kind=kOutput, calls=%fused_computation.110 | convolution fusion | flops 29163596 | bytes 11792520 | tf_op jit(solution)/shard_map/fg,gmxyz->fmxyz/dot_general | solution.py:84
  181.9 16.3 %collective-permute-done.18 = f32[5,16,1,8,128]{4,0,3,2,1:T(8,128)S(1)} collective-permute-done((f32[5,16,1,8,128]{4,0,3,2,1:T(8,128)S(1)}, f32[5,16,1,8,128]{4,0,3,2,1:T(8,128)S(1)}, u32[]{:S(2)}, u32[]{:S(2)}) %collective-permute-start.18) | collective-permute-done | bytes 327712 | tf_op jit(solution)/shard_map/ppermute | solution.py:51
  198.3 7.1 %collective-permute-start.20 = (f32[5,16,6,1,128]{4,0,3,2,1:T(8,128)S(1)}, f32[5,16,6,1,128]{4,0,3,2,1:T(8,128)S(1)}, u32[]{:S(2)}, u32[]{:S(2)}) collective-permute-start(f32[5,16,6,1,128]{4,0,3,2,1:T(8,128)S(1)} %get-tuple-element.16), channel_id=1, source_target_pairs={{0,1},{1,2},{2,3},{4,5},{5,6},{6,7},{8,9},{9,10},{10,11},{12,13},{... | collective-permute-start | bytes 737288 | tf_op jit(solution)/shard_map/ppermute | solution.py:51
  212.3 8.5 %fusion.6 = f32[5,16,4,8,128]{4,0,3,2,1:T(8,128)S(1)} fusion(f32[5,16,4,8,128]{4,0,3,2,1:T(8,128)S(1)} %get-tuple-element.65, f32[5,16,4,8,128]{4,0,3,2,1:T(8,128)S(1)} %fusion.39, f32[5,16,4,8,128]{4,0,3,2,1:T(8,128)S(1)} %fusion.41, f32[5,16,1,8,128]{4,0,3,2,1:T(8,128)S(1)} %collective-permute-done.17, ...), kind=kOutput, calls=%fused_computation.14 | convolution fusion | flops 32112716 | bytes 14413992 | tf_op jit(solution)/shard_map/fg,gmxyz->fmxyz/dot_general | solution.py:84
  238.0 13.0 %collective-permute-start.24 = (f32[5,16,6,1,128]{4,0,3,2,1:T(8,128)S(1)}, f32[5,16,6,1,128]{4,0,3,2,1:T(8,128)S(1)}, u32[]{:S(2)}, u32[]{:S(2)}) collective-permute-start(f32[5,16,6,1,128]{4,0,3,2,1:T(8,128)S(1)} %get-tuple-element.14), channel_id=1, source_target_pairs={{0,1},{1,2},{2,3},{4,5},{5,6},{6,7},{8,9},{9,10},{10,11},{12,13},{... | collective-permute-start | bytes 737288 | tf_op jit(solution)/shard_map/ppermute | solution.py:51
  257.9 6.0 %multiply_add_fusion.9 = (f32[5,16,4,8,128]{4,0,3,2,1:T(8,128)S(1)}, f32[5,16,4,8,128]{4,0,3,2,1:T(8,128)}) fusion(f32[5,16,4,8,128]{4,0,3,2,1:T(8,128)S(1)} %fusion.6, f32[8]{0:T(128)S(1)} %copy-done.18, f32[5,16,4,128]{3,0,2,1:T(8,128)S(1)} %broadcast_multiply_fusion, f32[4,8,128]{2,1,0:T(8,128)S(1)} %copy-done.8, ...), kind=kOutput, calls=%fused_computation.96 | convolution fusion | flops 29163596 | bytes 10481800 | tf_op jit(solution)/shard_map/fg,gmxyz->fmxyz/dot_general | solution.py:84
  275.6 6.3 %collective-permute-done.25 = f32[5,16,1,8,128]{4,0,3,2,1:T(8,128)S(1)} collective-permute-done((f32[5,16,1,8,128]{4,0,3,2,1:T(8,128)S(1)}, f32[5,16,1,8,128]{4,0,3,2,1:T(8,128)S(1)}, u32[]{:S(2)}, u32[]{:S(2)}) %collective-permute-start.25) | collective-permute-done | bytes 327712 | tf_op jit(solution)/shard_map/ppermute | solution.py:52
  282.0 12.1 %collective-permute-start.28 = (f32[5,16,6,1,128]{4,0,3,2,1:T(8,128)S(1)}, f32[5,16,6,1,128]{4,0,3,2,1:T(8,128)S(1)}, u32[]{:S(2)}, u32[]{:S(2)}) collective-permute-start(f32[5,16,6,1,128]{4,0,3,2,1:T(8,128)S(1)} %get-tuple-element.12), channel_id=1, source_target_pairs={{0,1},{1,2},{2,3},{4,5},{5,6},{6,7},{8,9},{9,10},{10,11},{12,13},{... | collective-permute-start | bytes 737288 | tf_op jit(solution)/shard_map/ppermute | solution.py:51
  317.3 7.2 %collective-permute-done.29 = f32[5,16,1,8,128]{4,0,3,2,1:T(8,128)S(1)} collective-permute-done((f32[5,16,1,8,128]{4,0,3,2,1:T(8,128)S(1)}, f32[5,16,1,8,128]{4,0,3,2,1:T(8,128)S(1)}, u32[]{:S(2)}, u32[]{:S(2)}) %collective-permute-start.29) | collective-permute-done | bytes 327712 | tf_op jit(solution)/shard_map/ppermute | solution.py:52
  324.6 11.2 %collective-permute-start.32 = (f32[5,16,6,1,128]{4,0,3,2,1:T(8,128)S(1)}, f32[5,16,6,1,128]{4,0,3,2,1:T(8,128)S(1)}, u32[]{:S(2)}, u32[]{:S(2)}) collective-permute-start(f32[5,16,6,1,128]{4,0,3,2,1:T(8,128)S(1)} %get-tuple-element.10), channel_id=1, source_target_pairs={{0,1},{1,2},{2,3},{4,5},{5,6},{6,7},{8,9},{9,10},{10,11},{12,13},{... | collective-permute-start | bytes 737288 | tf_op jit(solution)/shard_map/ppermute | solution.py:51
  343.0 6.1 %multiply_add_fusion.7 = (f32[5,16,4,8,128]{4,0,3,2,1:T(8,128)S(1)}, f32[5,16,4,8,128]{4,0,3,2,1:T(8,128)}) fusion(f32[5,16,4,8,128]{4,0,3,2,1:T(8,128)S(1)} %fusion.6, f32[8]{0:T(128)S(1)} %copy-done.20, f32[5,16,4,128]{3,0,2,1:T(8,128)S(1)} %broadcast_multiply_fusion, f32[5,16,4,8,128]{4,0,3,2,1:T(8,128)S(1)} %get-tuple-element.69, ...), kind=kOutput, calls=%fused_computation.82 | convolution fusion | flops 29163596 | bytes 11792520 | tf_op jit(solution)/shard_map/fg,gmxyz->fmxyz/dot_general | solution.py:84
  360.8 8.1 %collective-permute-done.33 = f32[5,16,1,8,128]{4,0,3,2,1:T(8,128)S(1)} collective-permute-done((f32[5,16,1,8,128]{4,0,3,2,1:T(8,128)S(1)}, f32[5,16,1,8,128]{4,0,3,2,1:T(8,128)S(1)}, u32[]{:S(2)}, u32[]{:S(2)}) %collective-permute-start.33) | collective-permute-done | bytes 327712 | tf_op jit(solution)/shard_map/ppermute | solution.py:52
  369.0 10.3 %collective-permute-start.36 = (f32[5,16,6,1,128]{4,0,3,2,1:T(8,128)S(1)}, f32[5,16,6,1,128]{4,0,3,2,1:T(8,128)S(1)}, u32[]{:S(2)}, u32[]{:S(2)}) collective-permute-start(f32[5,16,6,1,128]{4,0,3,2,1:T(8,128)S(1)} %get-tuple-element.8), channel_id=1, source_target_pairs={{0,1},{1,2},{2,3},{4,5},{5,6},{6,7},{8,9},{9,10},{10,11},{12,13},{... | collective-permute-start | bytes 737288 | tf_op jit(solution)/shard_map/ppermute | solution.py:51
  387.5 7.5 %multiply_add_fusion.6 = f32[5,16,4,8,128]{4,0,3,2,1:T(8,128)S(1)} fusion(f32[5,16,4,8,128]{4,0,3,2,1:T(8,128)S(1)} %fusion.6, f32[5,16,4,8,128]{4,0,3,2,1:T(8,128)S(1)} %get-tuple-element.71, f32[5,16,4,8,128]{4,0,3,2,1:T(8,128)S(1)} %fusion.7, f32[5,16,4,8,128]{4,0,3,2,1:T(8,128)} %fusion.9, f32[5,16,1,8,128]{4,0,3,2,1:T(8,128)S(1)} %collective-permute-done.33, ...), kind=kOutput, calls=%fused_computation.75 | convolution fusion | flops 32112716 | bytes 14413992 | tf_op jit(solution)/shard_map/fg,gmxyz->fmxyz/dot_general | solution.py:84
  397.4 11.1 %fusion.87 = f32[2,16,2,16]{3,1,2,0:T(8,128)S(1)} fusion(f32[2,5,16,4,8,128]{5,1,4,3,2,0:T(8,128)S(1)} %get-tuple-element.7, f32[2,5,16,4,8,128,1]{5,1,4,3,2,0,6:T(8,128)S(1)} %get-tuple-element.6), kind=kOutput, calls=%fused_computation.150 | convolution fusion | flops 251658240 | bytes 5246976 | tf_op jit(solution)/shard_map/sfmxyz,tfnxyz->smtn/dot_general | solution.py:152
  408.7 49.3 %psum.7 = f32[32,32]{0,1:T(8,128)S(1)} all-reduce(f32[32,32]{0,1:T(8,128)S(1)} %reshape.86), channel_id=1, replica_groups=mesh['gx'=8,'gy'=4] {'gx','gy'}, use_global_device_ids=true, to_apply=%region_1.2 | all-reduce | flops 1024 | bytes 8192 | tf_op jit(solution)/shard_map/psum | solution.py:155
  (187 shorter events, 192.3 us)
Async XLA Ops:
  0.6 22.5 %collective-permute-start.4 = (f32[1,16,256]{2,1,0:T(8,128)}, f32[1,16,256]{2,1,0:T(8,128)S(1)}, u32[]{:S(2)}, u32[]{:S(2)}) collective-permute-start(f32[1,16,256]{2,1,0:T(8,128)} %bitcast.133), channel_id=1, source_target_pairs={{0,1},{1,0},{2,3},{3,2},{4,5},{5,4},{6,7},{7,6},{8,9},{9,8},{10,11... | collective-permute-start | bytes 49160 | tf_op jit(solution)/shard_map/ppermute | solution.py:30
  4.4 41.3 %collective-permute-start = (f32[5,16,1,8,128]{4,0,3,2,1:T(8,128)}, f32[5,16,1,8,128]{4,0,3,2,1:T(8,128)}, u32[]{:S(2)}, u32[]{:S(2)}) collective-permute-start(f32[5,16,1,8,128]{4,0,3,2,1:T(8,128)} %get-tuple-element.52), channel_id=1, source_target_pairs={{4,0},{8,4},{12,8},{16,12},{20,16},{24,20},{28,24},{5,1},{9,5},{13... | collective-permute-start | bytes 983048 | tf_op jit(solution)/shard_map/ppermute | solution.py:52
  5.7 38.0 %collective-permute-start.1 = (f32[5,16,1,8,128]{4,0,3,2,1:T(8,128)}, f32[5,16,1,8,128]{4,0,3,2,1:T(8,128)}, u32[]{:S(2)}, u32[]{:S(2)}) collective-permute-start(f32[5,16,1,8,128]{4,0,3,2,1:T(8,128)} %get-tuple-element.53), channel_id=1, source_target_pairs={{0,4},{4,8},{8,12},{12,16},{16,20},{20,24},{24,28},{1,5},{5,9},{9,... | collective-permute-start | bytes 983048 | tf_op jit(solution)/shard_map/ppermute | solution.py:51
  41.1 14.0 %collective-permute-start.8 = (f32[16,16,256]{2,1,0:T(8,128)S(1)}, f32[16,16,256]{2,1,0:T(8,128)S(1)}, u32[]{:S(2)}, u32[]{:S(2)}) collective-permute-start(f32[16,16,256]{2,1,0:T(8,128)S(1)} %bitcast.123), channel_id=1, source_target_pairs={{0,16},{1,17},{2,18},{3,19},{4,20},{5,21},{6,22},{7,23},{8,24},{9,... | collective-permute-start | bytes 786440 | tf_op jit(solution)/shard_map/ppermute | solution.py:30
  49.4 23.7 %collective-permute-start.3 = (f32[5,16,6,1,128]{4,0,3,2,1:T(8,128)}, f32[5,16,6,1,128]{4,0,3,2,1:T(8,128)}, u32[]{:S(2)}, u32[]{:S(2)}) collective-permute-start(f32[5,16,6,1,128]{4,0,3,2,1:T(8,128)} %get-tuple-element.22), channel_id=1, source_target_pairs={{0,1},{1,2},{2,3},{4,5},{5,6},{6,7},{8,9},{9,10},{10,11},{12,13},{... | collective-permute-start | bytes 737288 | tf_op jit(solution)/shard_map/ppermute | solution.py:51
  51.4 21.7 %collective-permute-start.2 = (f32[5,16,6,1,128]{4,0,3,2,1:T(8,128)}, f32[5,16,6,1,128]{4,0,3,2,1:T(8,128)}, u32[]{:S(2)}, u32[]{:S(2)}) collective-permute-start(f32[5,16,6,1,128]{4,0,3,2,1:T(8,128)} %get-tuple-element.23), channel_id=1, source_target_pairs={{1,0},{2,1},{3,2},{5,4},{6,5},{7,6},{9,8},{10,9},{11,10},{13,12},{... | collective-permute-start | bytes 737288 | tf_op jit(solution)/shard_map/ppermute | solution.py:52
  86.9 27.1 %collective-permute-start.10 = (f32[5,16,1,8,128]{4,0,3,2,1:T(8,128)S(1)}, f32[5,16,1,8,128]{4,0,3,2,1:T(8,128)S(1)}, u32[]{:S(2)}, u32[]{:S(2)}) collective-permute-start(f32[5,16,1,8,128]{4,0,3,2,1:T(8,128)S(1)} %get-tuple-element.48), channel_id=1, source_target_pairs={{0,4},{4,8},{8,12},{12,16},{16,20},{20,24},{24,28},{1,5},{5,9},{9,... | collective-permute-start | bytes 983048 | tf_op jit(solution)/shard_map/ppermute | solution.py:51
  91.4 22.6 %collective-permute-start.9 = (f32[5,16,1,8,128]{4,0,3,2,1:T(8,128)S(1)}, f32[5,16,1,8,128]{4,0,3,2,1:T(8,128)S(1)}, u32[]{:S(2)}, u32[]{:S(2)}) collective-permute-start(f32[5,16,1,8,128]{4,0,3,2,1:T(8,128)S(1)} %get-tuple-element.49), channel_id=1, source_target_pairs={{4,0},{8,4},{12,8},{16,12},{20,16},{24,20},{28,24},{5,1},{9,5},{13... | collective-permute-start | bytes 983048 | tf_op jit(solution)/shard_map/ppermute | solution.py:52
  130.5 23.4 %collective-permute-start.14 = (f32[5,16,1,8,128]{4,0,3,2,1:T(8,128)S(1)}, f32[5,16,1,8,128]{4,0,3,2,1:T(8,128)S(1)}, u32[]{:S(2)}, u32[]{:S(2)}) collective-permute-start(f32[5,16,1,8,128]{4,0,3,2,1:T(8,128)S(1)} %get-tuple-element.44), channel_id=1, source_target_pairs={{0,4},{4,8},{8,12},{12,16},{16,20},{20,24},{24,28},{1,5},{5,9},{9,... | collective-permute-start | bytes 983048 | tf_op jit(solution)/shard_map/ppermute | solution.py:51
  134.9 19.0 %collective-permute-start.13 = (f32[5,16,1,8,128]{4,0,3,2,1:T(8,128)S(1)}, f32[5,16,1,8,128]{4,0,3,2,1:T(8,128)S(1)}, u32[]{:S(2)}, u32[]{:S(2)}) collective-permute-start(f32[5,16,1,8,128]{4,0,3,2,1:T(8,128)S(1)} %get-tuple-element.45), channel_id=1, source_target_pairs={{4,0},{8,4},{12,8},{16,12},{20,16},{24,20},{28,24},{5,1},{9,5},{13... | collective-permute-start | bytes 983048 | tf_op jit(solution)/shard_map/ppermute | solution.py:52
  175.3 22.9 %collective-permute-start.18 = (f32[5,16,1,8,128]{4,0,3,2,1:T(8,128)S(1)}, f32[5,16,1,8,128]{4,0,3,2,1:T(8,128)S(1)}, u32[]{:S(2)}, u32[]{:S(2)}) collective-permute-start(f32[5,16,1,8,128]{4,0,3,2,1:T(8,128)S(1)} %get-tuple-element.40), channel_id=1, source_target_pairs={{0,4},{4,8},{8,12},{12,16},{16,20},{20,24},{24,28},{1,5},{5,9},{9,... | collective-permute-start | bytes 983048 | tf_op jit(solution)/shard_map/ppermute | solution.py:51
  179.7 18.4 %collective-permute-start.17 = (f32[5,16,1,8,128]{4,0,3,2,1:T(8,128)S(1)}, f32[5,16,1,8,128]{4,0,3,2,1:T(8,128)S(1)}, u32[]{:S(2)}, u32[]{:S(2)}) collective-permute-start(f32[5,16,1,8,128]{4,0,3,2,1:T(8,128)S(1)} %get-tuple-element.41), channel_id=1, source_target_pairs={{4,0},{8,4},{12,8},{16,12},{20,16},{24,20},{28,24},{5,1},{9,5},{13... | collective-permute-start | bytes 983048 | tf_op jit(solution)/shard_map/ppermute | solution.py:52
  220.9 11.5 %collective-permute-start.22 = (f32[5,16,1,8,128]{4,0,3,2,1:T(8,128)S(1)}, f32[5,16,1,8,128]{4,0,3,2,1:T(8,128)S(1)}, u32[]{:S(2)}, u32[]{:S(2)}) collective-permute-start(f32[5,16,1,8,128]{4,0,3,2,1:T(8,128)S(1)} %get-tuple-element.36), channel_id=1, source_target_pairs={{0,4},{4,8},{8,12},{12,16},{16,20},{20,24},{24,28},{1,5},{5,9},{9,... | collective-permute-start | bytes 983048 | tf_op jit(solution)/shard_map/ppermute | solution.py:51
  225.3 12.6 %collective-permute-start.21 = (f32[5,16,1,8,128]{4,0,3,2,1:T(8,128)S(1)}, f32[5,16,1,8,128]{4,0,3,2,1:T(8,128)S(1)}, u32[]{:S(2)}, u32[]{:S(2)}) collective-permute-start(f32[5,16,1,8,128]{4,0,3,2,1:T(8,128)S(1)} %get-tuple-element.37), channel_id=1, source_target_pairs={{4,0},{8,4},{12,8},{16,12},{20,16},{24,20},{28,24},{5,1},{9,5},{13... | collective-permute-start | bytes 983048 | tf_op jit(solution)/shard_map/ppermute | solution.py:52
  238.0 17.4 %collective-permute-start.24 = (f32[5,16,6,1,128]{4,0,3,2,1:T(8,128)S(1)}, f32[5,16,6,1,128]{4,0,3,2,1:T(8,128)S(1)}, u32[]{:S(2)}, u32[]{:S(2)}) collective-permute-start(f32[5,16,6,1,128]{4,0,3,2,1:T(8,128)S(1)} %get-tuple-element.14), channel_id=1, source_target_pairs={{0,1},{1,2},{2,3},{4,5},{5,6},{6,7},{8,9},{9,10},{10,11},{12,13},{... | collective-permute-start | bytes 737288 | tf_op jit(solution)/shard_map/ppermute | solution.py:51
  264.1 11.6 %collective-permute-start.26 = (f32[5,16,1,8,128]{4,0,3,2,1:T(8,128)S(1)}, f32[5,16,1,8,128]{4,0,3,2,1:T(8,128)S(1)}, u32[]{:S(2)}, u32[]{:S(2)}) collective-permute-start(f32[5,16,1,8,128]{4,0,3,2,1:T(8,128)S(1)} %get-tuple-element.32), channel_id=1, source_target_pairs={{0,4},{4,8},{8,12},{12,16},{16,20},{20,24},{24,28},{1,5},{5,9},{9,... | collective-permute-start | bytes 983048 | tf_op jit(solution)/shard_map/ppermute | solution.py:51
  268.4 13.5 %collective-permute-start.25 = (f32[5,16,1,8,128]{4,0,3,2,1:T(8,128)S(1)}, f32[5,16,1,8,128]{4,0,3,2,1:T(8,128)S(1)}, u32[]{:S(2)}, u32[]{:S(2)}) collective-permute-start(f32[5,16,1,8,128]{4,0,3,2,1:T(8,128)S(1)} %get-tuple-element.33), channel_id=1, source_target_pairs={{4,0},{8,4},{12,8},{16,12},{20,16},{24,20},{28,24},{5,1},{9,5},{13... | collective-permute-start | bytes 983048 | tf_op jit(solution)/shard_map/ppermute | solution.py:52
  282.0 16.7 %collective-permute-start.28 = (f32[5,16,6,1,128]{4,0,3,2,1:T(8,128)S(1)}, f32[5,16,6,1,128]{4,0,3,2,1:T(8,128)S(1)}, u32[]{:S(2)}, u32[]{:S(2)}) collective-permute-start(f32[5,16,6,1,128]{4,0,3,2,1:T(8,128)S(1)} %get-tuple-element.12), channel_id=1, source_target_pairs={{0,1},{1,2},{2,3},{4,5},{5,6},{6,7},{8,9},{9,10},{10,11},{12,13},{... | collective-permute-start | bytes 737288 | tf_op jit(solution)/shard_map/ppermute | solution.py:51
  305.8 11.5 %collective-permute-start.30 = (f32[5,16,1,8,128]{4,0,3,2,1:T(8,128)S(1)}, f32[5,16,1,8,128]{4,0,3,2,1:T(8,128)S(1)}, u32[]{:S(2)}, u32[]{:S(2)}) collective-permute-start(f32[5,16,1,8,128]{4,0,3,2,1:T(8,128)S(1)} %get-tuple-element.28), channel_id=1, source_target_pairs={{0,4},{4,8},{8,12},{12,16},{16,20},{20,24},{24,28},{1,5},{5,9},{9,... | collective-permute-start | bytes 983048 | tf_op jit(solution)/shard_map/ppermute | solution.py:51
  310.1 14.4 %collective-permute-start.29 = (f32[5,16,1,8,128]{4,0,3,2,1:T(8,128)S(1)}, f32[5,16,1,8,128]{4,0,3,2,1:T(8,128)S(1)}, u32[]{:S(2)}, u32[]{:S(2)}) collective-permute-start(f32[5,16,1,8,128]{4,0,3,2,1:T(8,128)S(1)} %get-tuple-element.29), channel_id=1, source_target_pairs={{4,0},{8,4},{12,8},{16,12},{20,16},{24,20},{28,24},{5,1},{9,5},{13... | collective-permute-start | bytes 983048 | tf_op jit(solution)/shard_map/ppermute | solution.py:52
  324.6 15.5 %collective-permute-start.32 = (f32[5,16,6,1,128]{4,0,3,2,1:T(8,128)S(1)}, f32[5,16,6,1,128]{4,0,3,2,1:T(8,128)S(1)}, u32[]{:S(2)}, u32[]{:S(2)}) collective-permute-start(f32[5,16,6,1,128]{4,0,3,2,1:T(8,128)S(1)} %get-tuple-element.10), channel_id=1, source_target_pairs={{0,1},{1,2},{2,3},{4,5},{5,6},{6,7},{8,9},{9,10},{10,11},{12,13},{... | collective-permute-start | bytes 737288 | tf_op jit(solution)/shard_map/ppermute | solution.py:51
  349.2 11.6 %collective-permute-start.34 = (f32[5,16,1,8,128]{4,0,3,2,1:T(8,128)S(1)}, f32[5,16,1,8,128]{4,0,3,2,1:T(8,128)S(1)}, u32[]{:S(2)}, u32[]{:S(2)}) collective-permute-start(f32[5,16,1,8,128]{4,0,3,2,1:T(8,128)S(1)} %get-tuple-element.24), channel_id=1, source_target_pairs={{0,4},{4,8},{8,12},{12,16},{16,20},{20,24},{24,28},{1,5},{5,9},{9,... | collective-permute-start | bytes 983048 | tf_op jit(solution)/shard_map/ppermute | solution.py:51
  353.6 15.3 %collective-permute-start.33 = (f32[5,16,1,8,128]{4,0,3,2,1:T(8,128)S(1)}, f32[5,16,1,8,128]{4,0,3,2,1:T(8,128)S(1)}, u32[]{:S(2)}, u32[]{:S(2)}) collective-permute-start(f32[5,16,1,8,128]{4,0,3,2,1:T(8,128)S(1)} %get-tuple-element.25), channel_id=1, source_target_pairs={{4,0},{8,4},{12,8},{16,12},{20,16},{24,20},{28,24},{5,1},{9,5},{13... | collective-permute-start | bytes 983048 | tf_op jit(solution)/shard_map/ppermute | solution.py:52
  369.0 14.4 %collective-permute-start.36 = (f32[5,16,6,1,128]{4,0,3,2,1:T(8,128)S(1)}, f32[5,16,6,1,128]{4,0,3,2,1:T(8,128)S(1)}, u32[]{:S(2)}, u32[]{:S(2)}) collective-permute-start(f32[5,16,6,1,128]{4,0,3,2,1:T(8,128)S(1)} %get-tuple-element.8), channel_id=1, source_target_pairs={{0,1},{1,2},{2,3},{4,5},{5,6},{6,7},{8,9},{9,10},{10,11},{12,13},{... | collective-permute-start | bytes 737288 | tf_op jit(solution)/shard_map/ppermute | solution.py:51
  (35 other events, 221.2 us)
